TPU v7x, 32 devices: a whole 2x2x4 slice. The times are simulated.
32 devices in a mesh: dp: 8 (over z, y), section: 4 (over x, core).
Axes of the slice: x: 2, y: 2, z: 4, core: 2. Of those that a mesh axis runs over, the one named last changes fastest.
Arguments:
- patches: bfloat16 [64, 197, 1024], P('dp'), may hold values from -6 to 6
- ln1_gain: float32 [4, 1024], P('section'), may hold values from 0.5 to 1.5
- w_qkv: bfloat16 [4, 1024, 3072], P('section'), may hold values from -1 to 1
- w_out: bfloat16 [4, 1024, 1024], P('section'), may hold values from -0.1875 to 0.1875
- ln2_gain: float32 [4, 1024], P('section'), may hold values from 0.5 to 1.5
- w_fc1: bfloat16 [4, 1024, 2048], P('section'), may hold values from -0.1875 to 0.1875
- w_fc2: bfloat16 [4, 2048, 1024], P('section'), may hold values from -0.125 to 0.125
- final_norm_gain: float32 [1024], replicated, may hold values from 0.5 to 1.5
- w_head: bfloat16 [1024, 256], replicated, may hold values from -0.1875 to 0.1875
- online_embeddings: bfloat16 [64, 256], P('dp'), may hold values from -60 to 60
- queue: bfloat16 [32768, 256], P(('dp', 'section')), may hold values from -1 to 1, as said below
- owner: int32 [64], replicated, may hold values from 0 to 63, each once
- pointer: int32 [8], P('dp'), may hold values from 0 to 4088
Outputs:
- momentum_embeddings: bfloat16 [64, 256], P('dp')
- query_loss: float32 [64], P('dp')
- total_loss: float32 [], replicated
- new_queue: bfloat16 [32768, 256], P(('dp', 'section'))
Inputs may be any that keep to these rules, and one draw needn't show every extreme that they name: `queue`: every row has Euclidean norm below 1. Each value appears once: key j goes to group owner[j] // 8, so every group receives exactly 8 keys. `pointer`: first row of the group's shard where its new keys are written.
All inputs are finite; a program needn't handle non-finite values.
Results may differ from a plain program's by a relative error of at most 0.02.
Values may be sent and summed in bfloat16 or wider, within the bound.
A program may use at most 128 MiB of HBM per device.

v0:
```python
import functools
import math

import jax
import jax.numpy as jnp
from jax import lax
from jax.experimental import pallas as pl
from jax.experimental.pallas import tpu as pltpu
from jax.sharding import PartitionSpec as P

HEAD_DIM = 64


contrastive_sharpness = 0.2


def broadcast(value, axis, source):
    kept = jnp.where(lax.axis_index(axis) == source, value, 0).astype(value.dtype)
    return lax.psum(kept, axis)


def layer_norm(values, gain):
    center = values - jnp.mean(values, axis=-1, keepdims=True)
    spread = jnp.mean(center * center, axis=-1, keepdims=True)
    return center * lax.rsqrt(spread + 1e-06) * gain


def rounded_up(value, step):
    return (value + step - 1) // step * step


def gelu(x):
    return 0.5 * x * (1.0 + lax.erf(x * math.sqrt(0.5)))


def column_loop(total, tile, body):
    @pl.loop(0, total // tile)
    def _(step):
        body(pl.ds(pl.multiple_of(step * tile, tile), tile))


def attend(qkv_buf, c_buf, toks, width):
    rows = c_buf.shape[0]
    pair = 2 * HEAD_DIM
    lane = lax.broadcasted_iota(jnp.int32, (rows, pair), 1)
    first = lane < HEAD_DIM
    key_place = lax.broadcasted_iota(jnp.int32, (2 * rows, rows), 1)
    factor = math.log2(math.e) / math.sqrt(HEAD_DIM)

    def one_pair(columns, k_columns, v_columns):
        q = qkv_buf[:, columns]
        zero = jnp.zeros_like(q)
        q_both = jnp.concatenate([jnp.where(first, q, zero), jnp.where(first, zero, q)], axis=0)
        k = qkv_buf[:, k_columns]
        scores = lax.dot_general(
            q_both, k, (((1,), (1,)), ((), ())), preferred_element_type=jnp.float32
        )
        scores = jnp.where(key_place < toks, scores, -jnp.inf)
        peak = jnp.max(scores, axis=1, keepdims=True)
        expo = jnp.exp2((scores - peak) * factor)
        total = jnp.sum(expo, axis=1, keepdims=True)
        c = jnp.dot(
            expo.astype(jnp.bfloat16), qkv_buf[:, v_columns], preferred_element_type=jnp.float32
        )
        c = c / total
        c_buf[:, columns] = jnp.where(first, c[:rows], c[rows:]).astype(jnp.bfloat16)

    for at in range(0, width, pair):
        one_pair(
            pl.ds(at, pair),
            pl.ds(width + at, pair),
            pl.ds(2 * width + at, pair),
        )


def pipeline_kernel(
    sections,
    toks,
    patches,
    gain_one,
    gain_two,
    w_qkv,
    w_out,
    w_fc1,
    w_fc2,
    class_rows,
    v_qkv,
    v_out,
    v_fc1,
    v_fc2,
    raw,
    came,
    leaving,
    a_buf,
    qkv_buf,
    c_buf,
    r_buf,
    u_buf,
    weight_sem,
    raw_sem,
    send_sem,
    recv_sem,
):
    me = lax.axis_index("section")
    images, rows, width = came.shape
    hidden_units = v_fc1.shape[1]
    loads = [
        pltpu.make_async_copy(source.at[0], target, weight_sem.at[place])
        for place, (source, target) in enumerate(
            ((w_qkv, v_qkv), (w_out, v_out), (w_fc1, v_fc1), (w_fc2, v_fc2))
        )
    ]

    def raw_load(image):
        return pltpu.make_async_copy(patches.at[image], raw.at[image], raw_sem.at[image])

    @pl.when(me == 0)
    def _():
        raw_load(0).start()

    loads[0].start()
    for load in loads[1:]:
        load.start()

    @pl.when(me == 0)
    def _():
        for image in range(1, images):
            raw_load(image).start()

    barrier = pltpu.get_barrier_semaphore()

    @pl.when(me > 0)
    def _():
        pl.semaphore_signal(
            barrier, inc=1, device_id={"section": me - 1}, device_id_type=pl.DeviceIdType.MESH
        )

    @pl.when(me < sections - 1)
    def _():
        pl.semaphore_signal(
            barrier, inc=1, device_id={"section": me + 1}, device_id_type=pl.DeviceIdType.MESH
        )

    inner = jnp.logical_and(me > 0, me < sections - 1)

    @pl.when(inner)
    def _():
        pl.semaphore_wait(barrier, 2)

    @pl.when(jnp.logical_not(inner))
    def _():
        pl.semaphore_wait(barrier, 1)

    def handing(image):
        return pltpu.make_async_remote_copy(
            src_ref=leaving.at[image],
            dst_ref=came.at[image],
            send_sem=send_sem.at[image],
            recv_sem=recv_sem.at[image],
            device_id={"section": jnp.minimum(me + 1, sections - 1)},
            device_id_type=pl.DeviceIdType.MESH,
        )

    @pl.loop(0, images)
    def _(image):
        @pl.when(me == 0)
        def _():
            raw_load(image).wait()
            came[image, toks // 16 * 16 :, :] = jnp.zeros(
                (rows - toks // 16 * 16, width), jnp.bfloat16
            )
            came[image, 0:toks, :] = raw[image]

        @pl.when(me > 0)
        def _():
            handing(image).wait_recv()

        def arrive(place):
            @pl.when(image == 0)
            def _():
                loads[place].wait()

        a_buf[...] = layer_norm(came[image].astype(jnp.float32), gain_one[...]).astype(jnp.bfloat16)
        arrive(0)

        def qkv_part(columns):
            qkv_buf[:, columns] = jnp.dot(
                a_buf[...], v_qkv[:, columns], preferred_element_type=jnp.float32
            ).astype(jnp.bfloat16)

        column_loop(3 * width, 512, qkv_part)
        attend(qkv_buf, c_buf, toks, width)
        arrive(1)

        def out_part(columns):
            r_buf[:, columns] = came[image, :, columns].astype(jnp.float32) + jnp.dot(
                c_buf[...], v_out[:, columns], preferred_element_type=jnp.float32
            )

        column_loop(width, 512, out_part)
        a_buf[...] = layer_norm(r_buf[...], gain_two[...]).astype(jnp.bfloat16)
        arrive(2)

        def fc1_part(columns):
            u_buf[:, columns] = gelu(
                jnp.dot(a_buf[...], v_fc1[:, columns], preferred_element_type=jnp.float32)
            ).astype(jnp.bfloat16)

        column_loop(hidden_units, 512, fc1_part)
        arrive(3)

        def fc2_part(columns):
            leaving[image, :, columns] = (
                r_buf[:, columns]
                + jnp.dot(u_buf[...], v_fc2[:, columns], preferred_element_type=jnp.float32)
            ).astype(jnp.bfloat16)

        column_loop(width, 512, fc2_part)

        @pl.when(me < sections - 1)
        def _():
            handing(image).start()

    for image in range(images):
        class_rows[image : image + 1, :] = leaving[image, 0:1, :]

    @pl.when(me < sections - 1)
    def _():
        for image in range(images):
            handing(image).wait_send()


def run_pipeline(patches, gain_one, w_qkv, w_out, gain_two, w_fc1, w_fc2):
    sections = lax.axis_size("section")
    images, toks, width = patches.shape
    rows = rounded_up(toks, 16)
    hidden_units = w_fc1.shape[2]
    bf16 = jnp.bfloat16
    whole = pl.BlockSpec(memory_space=pltpu.VMEM)
    hbm = pl.BlockSpec(memory_space=pl.ANY)
    flops = 2 * images * toks * (4 * width * width + 2 * width * hidden_units)
    return pl.pallas_call(
        functools.partial(pipeline_kernel, sections, toks),
        out_shape=jax.ShapeDtypeStruct((images, width), bf16),
        in_specs=[hbm, whole, whole, hbm, hbm, hbm, hbm],
        out_specs=whole,
        scratch_shapes=[
            pltpu.VMEM((width, 3 * width), bf16),
            pltpu.VMEM((width, width), bf16),
            pltpu.VMEM((width, hidden_units), bf16),
            pltpu.VMEM((hidden_units, width), bf16),
            pltpu.VMEM((images, toks, width), bf16),
            pltpu.VMEM((images, rows, width), bf16),
            pltpu.VMEM((images, rows, width), bf16),
            pltpu.VMEM((rows, width), bf16),
            pltpu.VMEM((rows, 3 * width), bf16),
            pltpu.VMEM((rows, width), bf16),
            pltpu.VMEM((rows, width), jnp.float32),
            pltpu.VMEM((rows, hidden_units), bf16),
            pltpu.SemaphoreType.DMA((4,)),
            pltpu.SemaphoreType.DMA((images,)),
            pltpu.SemaphoreType.DMA((images,)),
            pltpu.SemaphoreType.DMA((images,)),
        ],
        compiler_params=pltpu.CompilerParams(
            collective_id=0, has_side_effects=True, vmem_limit_bytes=52 * 1024 * 1024
        ),
        cost_estimate=pl.CostEstimate(flops=flops, bytes_accessed=2**24, transcendentals=2**22),
    )(patches, gain_one, gain_two, w_qkv, w_out, w_fc1, w_fc2)


def key_head(class_rows, final_norm_gain, w_head):
    normed = layer_norm(class_rows.astype(jnp.float32), final_norm_gain).astype(jnp.bfloat16)
    projected = jnp.dot(normed, w_head, preferred_element_type=jnp.float32)
    scale = lax.rsqrt(1.0 + jnp.sum(projected * projected, axis=1, keepdims=True))
    return (projected * scale).astype(jnp.bfloat16)


def on_device(
    patches,
    ln1_gain,
    w_qkv,
    w_out,
    ln2_gain,
    w_fc1,
    w_fc2,
    final_norm_gain,
    w_head,
    online_embeddings,
    queue,
    owner,
    pointer,
):
    sections = lax.axis_size("section")
    section_index = lax.axis_index("section")
    group_index = lax.axis_index("dp")
    group_images = patches.shape[0]
    finished = run_pipeline(patches, ln1_gain, w_qkv, w_out, ln2_gain, w_fc1, w_fc2)
    resident_embeddings = key_head(finished, final_norm_gain, w_head)
    momentum_embeddings = broadcast(resident_embeddings, "section", sections - 1)
    query_rows_full = lax.all_gather(online_embeddings, "dp", axis=0, tiled=True)
    share = queue.shape[0]
    similarity_matrix = (
        jnp.einsum("tw,fw->tf", query_rows_full, queue, preferred_element_type=jnp.float32)
        / contrastive_sharpness
    )
    local_peak = jnp.max(similarity_matrix, axis=1)
    top = lax.pmax(local_peak, ("dp", "section"))
    total = lax.psum(jnp.sum(jnp.exp(similarity_matrix - top[:, None]), axis=1), ("dp", "section"))
    negative_all = top + jnp.log(total)
    negative = lax.dynamic_slice_in_dim(negative_all, group_index * group_images, group_images, 0)
    matching_similarity = (
        jnp.sum(
            online_embeddings.astype(jnp.float32) * momentum_embeddings.astype(jnp.float32), axis=1
        )
        / contrastive_sharpness
    )
    larger = jnp.maximum(negative, matching_similarity)
    query_loss = (
        larger
        + jnp.log(jnp.exp(negative - larger) + jnp.exp(matching_similarity - larger))
        - matching_similarity
    )
    loss_sum = lax.psum(jnp.sum(query_loss), "dp")
    total_loss = loss_sum / (group_images * lax.axis_size("dp"))
    every_key = lax.all_gather(momentum_embeddings, "dp", axis=0, tiled=True)
    wanted = group_index * group_images + jnp.arange(group_images, dtype=jnp.int32)
    selector = (owner[None, :] == wanted[:, None]).astype(jnp.bfloat16)
    incoming_keys = jnp.dot(selector, every_key, preferred_element_type=jnp.float32).astype(
        jnp.bfloat16
    )
    row_place = section_index * share + jnp.arange(share, dtype=jnp.int32)
    slot_index = row_place - pointer[0]
    placing = (slot_index[:, None] == jnp.arange(group_images, dtype=jnp.int32)[None, :]).astype(
        jnp.bfloat16
    )
    written = jnp.dot(placing, incoming_keys, preferred_element_type=jnp.float32).astype(
        jnp.bfloat16
    )
    inside = jnp.logical_and(slot_index >= 0, slot_index < group_images)
    new_queue = jnp.where(inside[:, None], written, queue)
    return (momentum_embeddings, query_loss, total_loss, new_queue)


def solution(mesh):
    placed = (
        P("dp", None, None),
        P("section", None),
        P("section", None, None),
        P("section", None, None),
        P("section", None),
        P("section", None, None),
        P("section", None, None),
        P(),
        P(),
        P("dp", None),
        P(("dp", "section"), None),
        P(),
        P("dp"),
    )
    return jax.shard_map(
        on_device,
        mesh=mesh,
        in_specs=placed,
        out_specs=(P("dp", None), P("dp"), P(), P(("dp", "section"), None)),
        check_vma=False,
    )
```

profile of v0, /device:TPU:0, one launch (start us, length us, event | category | flops | bytes accessed | tf_op | source)
XLA Modules:
  0.0 289.9 jit_solution(13307479956182413315)
XLA Ops:
  0.6 0.0 copy-start
  0.6 0.0 copy-start.1
  0.7 0.0 copy-start.2
  0.7 5.4 %copy.17.patches = bf16[8,197,1024]{2,1,0:T(8,128)(2,1)} copy(bf16[8,197,1024]{2,0,1:T(8,128)(2,1)} %param.13) | data formatting | bytes 6455296 | tf_op args[0]
  6.1 0.0 copy-done.1
  6.1 0.0 copy-done.2
  6.1 0.0 copy-start.7
  6.1 0.0 copy-start.3
  6.1 0.0 copy-start.6
  6.1 72.2 %shard_map.156 = bf16[8,1024]{1,0:T(8,128)(2,1)S(1)} custom-call(bf16[8,197,1024]{2,1,0:T(8,128)(2,1)} %copy.17.patches, f32[1,1024]{1,0:T(1,128)S(1)} %copy-done.1, f32[1,1024]{1,0:T(1,128)S(1)} %copy-done.2, bf16[1,1024,3072]{2,1,0:T(8,128)(2,1)} %w_qkv.1, bf16[1,1024,1024]{2,1,0:T(8,128)(2,1)} %w_out.1, bf16[1,1024,2048]{2,1,0:T(8,128)(2,1)} %w_fc1.1, ...), custom_call_target="tpu_custom_call" | custom-call | flops 26440892416 | bytes 16777216 | tf_op jit(solution)/shard_map/pallas_call | solution.py:242
  78.4 0.1 convert_reduce_fusion
  78.5 0.2 fusion.4
  78.7 0.0 copy-done
  78.7 0.0 copy-done.7
  78.7 0.3 multiply_reduce_fusion.1
  79.1 0.1 fusion.12
  79.2 40.1 %psum.21 = bf16[8,256]{1,0:T(8,128)(2,1)S(1)} all-reduce(bf16[8,256]{1,0:T(8,128)(2,1)S(1)} %fusion.12), channel_id=1, replica_groups=mesh['dp'=8,'section'=4] {'section'}, use_global_device_ids=true, to_apply=%region_3.4 | all-reduce | flops 2048 | bytes 8192 | tf_op jit(solution)/shard_map/psum | solution.py:19
  119.2 0.0 copy-done.5
  119.3 0.0 copy-start.4
  119.3 0.1 multiply_reduce_fusion
  119.4 32.4 %all_gather.6 = bf16[64,256]{1,0:T(8,128)(2,1)S(1)} all-gather(bf16[8,256]{1,0:T(8,128)(2,1)S(1)} %copy-done.5), channel_id=1, replica_groups=mesh['dp'=8,'section'=4] {'dp'}, dimensions={0}, use_global_device_ids=true | all-gather | bytes 36864 | tf_op jit(solution)/shard_map/all_gather | solution.py:301
  151.8 0.0 copy-done.3
  151.8 0.4 fusion.21
  152.2 38.5 %pmax.7 = f32[64]{0:T(128)S(1)} all-reduce(f32[64]{0:T(128)S(1)} %get-tuple-element.8), channel_id=1, replica_groups=mesh['dp'=8,'section'=4] {'dp','section'}, use_global_device_ids=true, to_apply=%region_5.6 | all-reduce | flops 64 | bytes 512 | tf_op jit(solution)/shard_map/pmax | solution.py:308
  190.7 0.2 exponential_reduce_fusion
  190.9 41.6 %psum.22 = f32[64]{0:T(128)S(1)} all-reduce(f32[64]{0:T(128)S(1)} %exponential_reduce_fusion), channel_id=1, replica_groups=mesh['dp'=8,'section'=4] {'dp','section'}, use_global_device_ids=true, to_apply=%region_7.8 | all-reduce | flops 64 | bytes 512 | tf_op jit(solution)/shard_map/psum | solution.py:309
  232.6 1.2 fusion.20
  233.8 21.7 %psum.23 = f32[]{:T(128)} all-reduce(f32[]{:T(128)} %get-tuple-element.4), channel_id=1, replica_groups=mesh['dp'=8,'section'=4] {'dp'}, use_global_device_ids=true, to_apply=%region_10.11 | all-reduce | flops 1 | bytes 8 | tf_op jit(solution)/shard_map/psum | solution.py:324
  256.1 30.6 %all_gather.7 = bf16[64,256]{1,0:T(8,128)(2,1)S(1)} all-gather(bf16[8,256]{1,0:T(8,128)(2,1)S(1)} %psum.21), channel_id=1, replica_groups=mesh['dp'=8,'section'=4] {'dp'}, dimensions={0}, use_global_device_ids=true | all-gather | bytes 36864 | tf_op jit(solution)/shard_map/all_gather | solution.py:326
  287.4 0.0 copy-done.6
  287.5 1.3 fusion
  288.7 0.0 copy-done.4
  (8 shorter events, 0.0 us)
Async XLA Ops:
  0.6 78.1 %copy-start = (bf16[1024,256]{1,0:T(8,128)(2,1)S(1)}, bf16[1024,256]{1,0:T(8,128)(2,1)}, u32[]{:S(2)}) copy-start(bf16[1024,256]{1,0:T(8,128)(2,1)} %param.21) | copy-start | bytes 1572868
  0.6 5.4 %copy-start.1 = (f32[1,1024]{1,0:T(1,128)S(1)}, f32[1,1024]{1,0:T(1,128)}, u32[]{:S(2)}) copy-start(f32[1,1024]{1,0:T(1,128)} %gain_one.1) | copy-start | bytes 12292
  0.7 5.4 %copy-start.2 = (f32[1,1024]{1,0:T(1,128)S(1)}, f32[1,1024]{1,0:T(1,128)}, u32[]{:S(2)}) copy-start(f32[1,1024]{1,0:T(1,128)} %gain_two.1) | copy-start | bytes 12292
  6.1 72.6 %copy-start.7 = (f32[1024]{0:T(1024)S(1)}, f32[1024]{0:T(1024)}, u32[]{:S(2)}) copy-start(f32[1024]{0:T(1024)} %param.20) | copy-start | bytes 12292
  6.1 113.2 %copy-start.5 = (bf16[8,256]{1,0:T(8,128)(2,1)S(1)}, bf16[8,256]{1,0:T(8,128)(2,1)}, u32[]{:S(2)}) copy-start(bf16[8,256]{1,0:T(8,128)(2,1)} %param.22) | copy-start | bytes 12292
  6.1 145.7 %copy-start.3 = (bf16[1024,256]{1,0:T(8,128)(2,1)S(1)}, bf16[1024,256]{1,0:T(8,128)(2,1)}, u32[]{:S(2)}) copy-start(bf16[1024,256]{1,0:T(8,128)(2,1)} %param.23) | copy-start | bytes 1572868
  6.1 281.3 %copy-start.6 = (s32[64]{0:T(128)S(1)}, s32[64]{0:T(128)}, u32[]{:S(2)}) copy-start(s32[64]{0:T(128)} %param.24) | copy-start | bytes 772
  119.3 169.5 %copy-start.4 = (bf16[8,256]{1,0:T(8,128)(2,1)}, bf16[8,256]{1,0:T(8,128)(2,1)S(1)}, u32[]{:S(2)}) copy-start(bf16[8,256]{1,0:T(8,128)(2,1)S(1)} %psum.21) | copy-start | bytes 12292
where the time goes:
time: 290 us
  blocking collectives  205 us (71%)
  Pallas kernels  72.2 us (25%)
  local copies, waits for them, and re-layouts  5.47 us (2%)
  between operations  3.2 us (1%)
    pallas_call x1, Pallas kernels, run_pipeline(): pl.pallas_call(functools.partial(pipeline_kernel, sections, toks), out_sh...  72.2 us
    psum x1, blocking collectives, on_device(): lax.psum(jnp.sum(jnp.exp(similarity_matrix - top[:, None]), axis=1), ('dp...  41.6 us
    psum x1, blocking collectives, broadcast(): return lax.psum(kept, axis)  40.1 us
    pmax x1, blocking collectives, on_device(): top = lax.pmax(local_peak, ('dp', 'section'))  38.5 us
    all_gather x1, blocking collectives, on_device(): lax.all_gather(online_embeddings, 'dp', axis=0, tiled=True)  32.4 us
    all_gather x1, blocking collectives, on_device(): every_key = lax.all_gather(momentum_embeddings, 'dp', axis=0, tiled=True)  30.6 us
    psum x1, blocking collectives, on_device(): loss_sum = lax.psum(jnp.sum(query_loss), 'dp')  21.7 us

commit v1 on v0

--- a/solution.py
+++ b/solution.py
@@ -12,11 +12,6 @@
 
 
 contrastive_sharpness = 0.2
-
-
-def broadcast(value, axis, source):
-    kept = jnp.where(lax.axis_index(axis) == source, value, 0).astype(value.dtype)
-    return lax.psum(kept, axis)
 
 
 def layer_norm(values, gain):
@@ -76,7 +71,9 @@
 def pipeline_kernel(
     sections,
     toks,
+    groups,
     patches,
+    online,
     gain_one,
     gain_two,
     w_qkv,
@@ -84,6 +81,7 @@
     w_fc1,
     w_fc2,
     class_rows,
+    queries,
     v_qkv,
     v_out,
     v_fc1,
@@ -100,8 +98,12 @@
     raw_sem,
     send_sem,
     recv_sem,
+    q_buf,
+    q_send,
+    q_recv,
 ):
     me = lax.axis_index("section")
+    group = lax.axis_index("dp")
     images, rows, width = came.shape
     hidden_units = v_fc1.shape[1]
     loads = [
@@ -141,15 +143,36 @@
             barrier, inc=1, device_id={"section": me + 1}, device_id_type=pl.DeviceIdType.MESH
         )
 
+    for step in range(1, groups):
+        pl.semaphore_signal(
+            barrier,
+            inc=1,
+            device_id={"dp": lax.rem(group + step, groups)},
+            device_id_type=pl.DeviceIdType.MESH,
+        )
+
     inner = jnp.logical_and(me > 0, me < sections - 1)
 
     @pl.when(inner)
     def _():
-        pl.semaphore_wait(barrier, 2)
+        pl.semaphore_wait(barrier, groups + 1)
 
     @pl.when(jnp.logical_not(inner))
     def _():
-        pl.semaphore_wait(barrier, 1)
+        pl.semaphore_wait(barrier, groups)
+
+    def query_copy(step):
+        return pltpu.make_async_remote_copy(
+            src_ref=online,
+            dst_ref=q_buf.at[group],
+            send_sem=q_send.at[step],
+            recv_sem=q_recv.at[step],
+            device_id={"dp": lax.rem(group + step, groups)},
+            device_id_type=pl.DeviceIdType.MESH,
+        )
+
+    for step in range(1, groups):
+        query_copy(step).start()
 
     def handing(image):
         return pltpu.make_async_remote_copy(
@@ -224,14 +247,20 @@
     for image in range(images):
         class_rows[image : image + 1, :] = leaving[image, 0:1, :]
 
+    for step in range(1, groups):
+        query_copy(step).wait()
+    queries[...] = q_buf[...]
+    queries[group] = online[...]
+
     @pl.when(me < sections - 1)
     def _():
         for image in range(images):
             handing(image).wait_send()
 
 
-def run_pipeline(patches, gain_one, w_qkv, w_out, gain_two, w_fc1, w_fc2):
+def run_pipeline(patches, online, gain_one, w_qkv, w_out, gain_two, w_fc1, w_fc2):
     sections = lax.axis_size("section")
+    groups = lax.axis_size("dp")
     images, toks, width = patches.shape
     rows = rounded_up(toks, 16)
     hidden_units = w_fc1.shape[2]
@@ -240,10 +269,13 @@
     hbm = pl.BlockSpec(memory_space=pl.ANY)
     flops = 2 * images * toks * (4 * width * width + 2 * width * hidden_units)
     return pl.pallas_call(
-        functools.partial(pipeline_kernel, sections, toks),
-        out_shape=jax.ShapeDtypeStruct((images, width), bf16),
-        in_specs=[hbm, whole, whole, hbm, hbm, hbm, hbm],
-        out_specs=whole,
+        functools.partial(pipeline_kernel, sections, toks, groups),
+        out_shape=(
+            jax.ShapeDtypeStruct((images, width), bf16),
+            jax.ShapeDtypeStruct((groups,) + online.shape, bf16),
+        ),
+        in_specs=[hbm, whole, whole, whole, hbm, hbm, hbm, hbm],
+        out_specs=(whole, whole),
         scratch_shapes=[
             pltpu.VMEM((width, 3 * width), bf16),
             pltpu.VMEM((width, width), bf16),
@@ -261,12 +293,64 @@
             pltpu.SemaphoreType.DMA((images,)),
             pltpu.SemaphoreType.DMA((images,)),
             pltpu.SemaphoreType.DMA((images,)),
+            pltpu.VMEM((groups,) + online.shape, bf16),
+            pltpu.SemaphoreType.DMA((groups,)),
+            pltpu.SemaphoreType.DMA((groups,)),
         ],
         compiler_params=pltpu.CompilerParams(
             collective_id=0, has_side_effects=True, vmem_limit_bytes=52 * 1024 * 1024
         ),
         cost_estimate=pl.CostEstimate(flops=flops, bytes_accessed=2**24, transcendentals=2**22),
-    )(patches, gain_one, gain_two, w_qkv, w_out, w_fc1, w_fc2)
+    )(patches, online, gain_one, gain_two, w_qkv, w_out, w_fc1, w_fc2)
+
+
+def exchange_kernel(groups, sections, mine, everyone, held, send_sem, recv_sem):
+    group, me = lax.axis_index("dp"), lax.axis_index("section")
+    place = group * sections + me
+    peers = [
+        {"dp": lax.rem(group + i, groups), "section": lax.rem(me + j, sections)}
+        for i in range(groups)
+        for j in range(sections)
+    ][1:]
+    barrier = pltpu.get_barrier_semaphore()
+    for peer in peers:
+        pl.semaphore_signal(barrier, inc=1, device_id=peer, device_id_type=pl.DeviceIdType.MESH)
+    pl.semaphore_wait(barrier, len(peers))
+    copies = [
+        pltpu.make_async_remote_copy(
+            src_ref=mine,
+            dst_ref=held.at[place],
+            send_sem=send_sem.at[turn],
+            recv_sem=recv_sem.at[turn],
+            device_id=peer,
+            device_id_type=pl.DeviceIdType.MESH,
+        )
+        for turn, peer in enumerate(peers)
+    ]
+    for copy in copies:
+        copy.start()
+    for copy in copies:
+        copy.wait()
+    everyone[...] = held[...]
+    everyone[place] = mine[...]
+
+
+def exchange(mine):
+    groups, sections = lax.axis_size("dp"), lax.axis_size("section")
+    devices = groups * sections
+    whole = pl.BlockSpec(memory_space=pltpu.VMEM)
+    return pl.pallas_call(
+        functools.partial(exchange_kernel, groups, sections),
+        out_shape=jax.ShapeDtypeStruct((devices,) + mine.shape, mine.dtype),
+        in_specs=[whole],
+        out_specs=whole,
+        scratch_shapes=[
+            pltpu.VMEM((devices,) + mine.shape, mine.dtype),
+            pltpu.SemaphoreType.DMA((devices,)),
+            pltpu.SemaphoreType.DMA((devices,)),
+        ],
+        compiler_params=pltpu.CompilerParams(collective_id=1, has_side_effects=True),
+    )(mine)
 
 
 def key_head(class_rows, final_norm_gain, w_head):
@@ -295,35 +379,53 @@
     section_index = lax.axis_index("section")
     group_index = lax.axis_index("dp")
     group_images = patches.shape[0]
-    finished = run_pipeline(patches, ln1_gain, w_qkv, w_out, ln2_gain, w_fc1, w_fc2)
+    groups = lax.axis_size("dp")
+    finished, query_blocks = run_pipeline(
+        patches, online_embeddings, ln1_gain, w_qkv, w_out, ln2_gain, w_fc1, w_fc2
+    )
+    kdim = online_embeddings.shape[1]
+    query_rows_full = query_blocks.reshape(groups * group_images, kdim)
     resident_embeddings = key_head(finished, final_norm_gain, w_head)
-    momentum_embeddings = broadcast(resident_embeddings, "section", sections - 1)
-    query_rows_full = lax.all_gather(online_embeddings, "dp", axis=0, tiled=True)
     share = queue.shape[0]
     similarity_matrix = (
         jnp.einsum("tw,fw->tf", query_rows_full, queue, preferred_element_type=jnp.float32)
         / contrastive_sharpness
     )
     local_peak = jnp.max(similarity_matrix, axis=1)
-    top = lax.pmax(local_peak, ("dp", "section"))
-    total = lax.psum(jnp.sum(jnp.exp(similarity_matrix - top[:, None]), axis=1), ("dp", "section"))
-    negative_all = top + jnp.log(total)
-    negative = lax.dynamic_slice_in_dim(negative_all, group_index * group_images, group_images, 0)
+    local_total = jnp.sum(jnp.exp(similarity_matrix - local_peak[:, None]), axis=1)
+    used = kdim + 2 * groups
+    message = jnp.concatenate(
+        [
+            resident_embeddings.astype(jnp.float32),
+            local_peak.reshape(groups, group_images).T,
+            local_total.reshape(groups, group_images).T,
+            jnp.zeros((group_images, rounded_up(used, 128) - used), jnp.float32),
+        ],
+        axis=1,
+    )
+    told = exchange(message)
+    every_key = told.reshape(groups, sections, group_images, -1)[:, sections - 1, :, :kdim]
+    every_key = every_key.reshape(groups * group_images, kdim).astype(jnp.bfloat16)
+    momentum_embeddings = lax.dynamic_slice_in_dim(
+        every_key, group_index * group_images, group_images, 0
+    )
+    peaks = told[:, :, kdim : kdim + groups]
+    totals = told[:, :, kdim + groups : kdim + 2 * groups]
+    top = jnp.max(peaks, axis=0)
+    total = jnp.sum(totals * jnp.exp(peaks - top[None]), axis=0)
+    negative = (top + jnp.log(total)).T
     matching_similarity = (
-        jnp.sum(
-            online_embeddings.astype(jnp.float32) * momentum_embeddings.astype(jnp.float32), axis=1
-        )
+        jnp.sum(query_rows_full.astype(jnp.float32) * every_key.astype(jnp.float32), axis=1)
         / contrastive_sharpness
-    )
+    ).reshape(groups, group_images)
     larger = jnp.maximum(negative, matching_similarity)
-    query_loss = (
+    every_loss = (
         larger
         + jnp.log(jnp.exp(negative - larger) + jnp.exp(matching_similarity - larger))
         - matching_similarity
     )
-    loss_sum = lax.psum(jnp.sum(query_loss), "dp")
-    total_loss = loss_sum / (group_images * lax.axis_size("dp"))
-    every_key = lax.all_gather(momentum_embeddings, "dp", axis=0, tiled=True)
+    query_loss = lax.dynamic_index_in_dim(every_loss, group_index, 0, keepdims=False)
+    total_loss = jnp.sum(every_loss) / (group_images * groups)
     wanted = group_index * group_images + jnp.arange(group_images, dtype=jnp.int32)
     selector = (owner[None, :] == wanted[:, None]).astype(jnp.bfloat16)
     incoming_keys = jnp.dot(selector, every_key, preferred_element_type=jnp.float32).astype(

time: 290 us -> 141 us (0.49)
  blocking collectives: 205 us -> 0 us
  Pallas kernels: 72.2 us -> 122 us
  other arithmetic: 1.96 us -> 4.92 us
    psum x3 -> x0, blocking collectives: 103 us -> none  [the longest x1 41.6 us: on_device(): lax.psum(jnp.sum(jnp.exp(similarity_matrix - top[:, None]), axis=1), ('dp...]
    all_gather x2 -> x0, blocking collectives: 63 us -> none  [the longest x1 32.4 us: on_device(): lax.all_gather(online_embeddings, 'dp', axis=0, tiled=True)]
    pallas_call x1 -> x2, Pallas kernels: 72.2 us -> 122 us  [the longest x1 75.4 us: run_pipeline(): pl.pallas_call(functools.partial(pipeline_kernel, sections, toks, groups)...]
    pmax x1 -> x0, blocking collectives: 38.5 us -> none  [on_device(): top = lax.pmax(local_peak, ('dp', 'section'))]
where the time goes in v1:
time: 141 us
  Pallas kernels  122 us (87%)
  local copies, waits for them, and re-layouts  8.05 us (6%)
  other arithmetic  4.92 us (3%)
  between operations  3.21 us (2%)
  matrix products  2.82 us (2%)
    pallas_call x1, Pallas kernels, run_pipeline(): pl.pallas_call(functools.partial(pipeline_kernel, sections, toks, groups)...  75.4 us
    pallas_call x1, Pallas kernels, exchange(): pl.pallas_call(functools.partial(exchange_kernel, groups, sections), out_...  46.2 us
    unnamed x15, local copies, waits for them, and re-layouts  5.46 us

profile of v1, /device:TPU:0, one launch (start us, length us, event | category | flops | bytes accessed | tf_op | source)
XLA Modules:
  0.0 140.7 jit_solution(5503058599831625963)
XLA Ops:
  0.6 0.0 copy-start
  0.6 0.0 copy-start.2
  0.7 0.0 copy-start.3
  0.7 0.0 copy-start.1
  0.7 5.4 %copy.30.patches = bf16[8,197,1024]{2,1,0:T(8,128)(2,1)} copy(bf16[8,197,1024]{2,0,1:T(8,128)(2,1)} %param.13) | data formatting | bytes 6455296 | tf_op args[0]
  6.1 0.0 copy-start.6
  6.1 0.0 copy-start.4
  6.1 0.0 copy-start.5
  6.1 75.4 %shard_map.156 = (bf16[8,1024]{1,0:T(8,128)(2,1)S(1)}, bf16[8,8,256]{2,1,0:T(8,128)(2,1)S(1)}) custom-call(bf16[8,197,1024]{2,1,0:T(8,128)(2,1)} %copy.30.patches, bf16[8,256]{1,0:T(8,128)(2,1)S(1)} %copy-done.1, f32[1,1024]{1,0:T(1,128)S(1)} %copy-done.2, f32[1,1024]{1,0:T(1,128)S(1)} %copy-done.3, bf16[1,1024,3072]{2,1,0:T(8,128)(2,1)} %w_qkv.1, ...), custom_call_target="tpu_custom_call" | custom-call | flops 26440892416 | bytes 16777216 | tf_op jit(solution)/shard_map/pallas_call | solution.py:271
  81.6 0.1 convert_reduce_fusion
  81.7 0.2 fusion.6
  81.9 0.3 multiply_reduce_fusion.1
  82.3 0.1 fusion.16
  82.4 0.4 fusion.32
  82.7 0.2 exponential_reduce_fusion
  83.0 0.1 reshape.67
  83.0 0.1 copy.32
  83.1 0.1 reshape.66
  83.2 0.1 copy.31
  83.3 0.1 pad.3.clone
  83.3 0.7 maximum_maximum_fusion.mine
  84.0 46.2 %shard_map.157 = f32[32,8,384]{2,1,0:T(8,128)} custom-call(f32[8,384]{1,0:T(8,128)} %maximum_maximum_fusion.mine), custom_call_target="tpu_custom_call" | custom-call | tf_op jit(solution)/shard_map/pallas_call | solution.py:342
  130.3 0.9 slice_reduce_fusion
  131.2 1.1 multiply_reduce_fusion
  132.3 0.9 fusion.3
  133.3 0.1 copy.34
  133.3 0.6 fusion.30
  134.0 0.7 dynamic-slice_reduce_fusion
  135.3 0.8 fusion.15
  136.1 0.6 constant_dynamic-slice_fusion
  137.4 0.0 copy-done.5
  137.4 2.1 %fusion = bf16[1024,256]{1,0:T(8,128)(2,1)} fusion(bf16[1024,256]{1,0:T(8,128)(2,1)S(1)} %copy-done.4, pred[1024]{0:T(1024)(128)(4,1)S(1)} %compare_and_fusion, s32[1024]{0:T(1024)S(1)} %add_subtract_fusion, s32[64]{0:T(128)S(1)} %copy-done.5, s32[8]{0:T(128)S(1)} %iota_add_fusion, f32[8,4,8,384]{3,2,1,0:T(8,128)} %bitcast.54), kind=kOutput, calls=%fused_computation.1 | convolution fusion | flops 4991488 | bytes 1086752 | tf_op jit(solution)/shard_map/dot_general | solution.py:439
  (13 shorter events, 0.1 us)
Async XLA Ops:
  0.6 81.3 %copy-start = (bf16[1024,256]{1,0:T(8,128)(2,1)S(1)}, bf16[1024,256]{1,0:T(8,128)(2,1)}, u32[]{:S(2)}) copy-start(bf16[1024,256]{1,0:T(8,128)(2,1)} %param.21) | copy-start | bytes 1572868
  0.6 5.5 %copy-start.2 = (f32[1,1024]{1,0:T(1,128)S(1)}, f32[1,1024]{1,0:T(1,128)}, u32[]{:S(2)}) copy-start(f32[1,1024]{1,0:T(1,128)} %gain_one.1) | copy-start | bytes 12292
  0.7 5.4 %copy-start.3 = (f32[1,1024]{1,0:T(1,128)S(1)}, f32[1,1024]{1,0:T(1,128)}, u32[]{:S(2)}) copy-start(f32[1,1024]{1,0:T(1,128)} %gain_two.1) | copy-start | bytes 12292
  0.7 5.4 %copy-start.1 = (bf16[8,256]{1,0:T(8,128)(2,1)S(1)}, bf16[8,256]{1,0:T(8,128)(2,1)}, u32[]{:S(2)}) copy-start(bf16[8,256]{1,0:T(8,128)(2,1)} %online.1) | copy-start | bytes 12292
  6.1 75.8 %copy-start.6 = (f32[1024]{0:T(1024)S(1)}, f32[1024]{0:T(1024)}, u32[]{:S(2)}) copy-start(f32[1024]{0:T(1024)} %param.20) | copy-start | bytes 12292
  6.1 76.2 %copy-start.4 = (bf16[1024,256]{1,0:T(8,128)(2,1)S(1)}, bf16[1024,256]{1,0:T(8,128)(2,1)}, u32[]{:S(2)}) copy-start(bf16[1024,256]{1,0:T(8,128)(2,1)} %param.23) | copy-start | bytes 1572868
  6.1 131.3 %copy-start.5 = (s32[64]{0:T(128)S(1)}, s32[64]{0:T(128)}, u32[]{:S(2)}) copy-start(s32[64]{0:T(128)} %param.24) | copy-start | bytes 772

commit v2 on v1

--- a/solution.py
+++ b/solution.py
@@ -29,9 +29,8 @@
 
 
 def column_loop(total, tile, body):
-    @pl.loop(0, total // tile)
-    def _(step):
-        body(pl.ds(pl.multiple_of(step * tile, tile), tile))
+    for at in range(0, total, tile):
+        body(pl.ds(at, tile))
 
 
 def attend(qkv_buf, c_buf, toks, width):
@@ -53,12 +52,12 @@
         scores = jnp.where(key_place < toks, scores, -jnp.inf)
         peak = jnp.max(scores, axis=1, keepdims=True)
         expo = jnp.exp2((scores - peak) * factor)
-        total = jnp.sum(expo, axis=1, keepdims=True)
-        c = jnp.dot(
-            expo.astype(jnp.bfloat16), qkv_buf[:, v_columns], preferred_element_type=jnp.float32
-        )
-        c = c / total
-        c_buf[:, columns] = jnp.where(first, c[:rows], c[rows:]).astype(jnp.bfloat16)
+        v = qkv_buf[:, v_columns]
+        v_and_one = jnp.concatenate([v, jnp.ones_like(v)], axis=1)
+        c = jnp.dot(expo.astype(jnp.bfloat16), v_and_one, preferred_element_type=jnp.float32)
+        above = jnp.where(first, c[:rows, :pair], c[rows:, :pair])
+        below = jnp.where(first, c[:rows, pair:], c[rows:, pair:])
+        c_buf[:, columns] = (above / below).astype(jnp.bfloat16)
 
     for at in range(0, width, pair):
         one_pair(

time: 141 us -> 116 us (0.82)
  Pallas kernels: 122 us -> 96.1 us
    pallas_call x1, Pallas kernels: 75.4 us -> 56.8 us  [run_pipeline(): pl.pallas_call(functools.partial(pipeline_kernel, sections, toks, groups)...]
    pallas_call x1, Pallas kernels: 46.2 us -> 39.3 us  [exchange(): pl.pallas_call(functools.partial(exchange_kernel, groups, sections), out_...]
where the time goes in v2:
time: 116 us; the launch traced here: 115 us
  Pallas kernels  96.1 us (83%)
  local copies, waits for them, and re-layouts  8.05 us (7%)
  other arithmetic  4.92 us (4%)
  between operations  3.21 us (3%)
  matrix products  2.82 us (2%)
    pallas_call x1, Pallas kernels, run_pipeline(): pl.pallas_call(functools.partial(pipeline_kernel, sections, toks, groups)...  56.8 us
    pallas_call x1, Pallas kernels, exchange(): pl.pallas_call(functools.partial(exchange_kernel, groups, sections), out_...  39.3 us
    unnamed x15, local copies, waits for them, and re-layouts  5.46 us

profile of v2, /device:TPU:0, one launch (start us, length us, event | category | flops | bytes accessed | tf_op | source)
XLA Modules:
  0.0 115.1 jit_solution(12526831545707607297)
XLA Ops:
  0.6 0.0 copy-start
  0.6 0.0 copy-start.2
  0.7 0.0 copy-start.3
  0.7 5.4 %copy.30.patches = bf16[8,197,1024]{2,1,0:T(8,128)(2,1)} copy(bf16[8,197,1024]{2,0,1:T(8,128)(2,1)} %param.13) | data formatting | bytes 6455296 | tf_op args[0]
  6.1 0.0 copy-done.3
  6.1 0.0 copy-start.6
  6.1 0.0 copy-start.4
  6.1 0.0 copy-start.5
  6.1 56.8 %shard_map.156 = (bf16[8,1024]{1,0:T(8,128)(2,1)S(1)}, bf16[8,8,256]{2,1,0:T(8,128)(2,1)S(1)}) custom-call(bf16[8,197,1024]{2,1,0:T(8,128)(2,1)} %copy.30.patches, bf16[8,256]{1,0:T(8,128)(2,1)S(1)} %copy-done.1, f32[1,1024]{1,0:T(1,128)S(1)} %copy-done.2, f32[1,1024]{1,0:T(1,128)S(1)} %copy-done.3, bf16[1,1024,3072]{2,1,0:T(8,128)(2,1)} %w_qkv.1, ...), custom_call_target="tpu_custom_call" | custom-call | flops 26440892416 | bytes 16777216 | tf_op jit(solution)/shard_map/pallas_call | solution.py:270
  63.0 0.1 convert_reduce_fusion
  63.1 0.2 fusion.6
  63.3 0.3 multiply_reduce_fusion.1
  63.7 0.1 fusion.16
  63.7 0.4 fusion.32
  64.1 0.2 exponential_reduce_fusion
  64.3 0.1 reshape.67
  64.4 0.1 copy.32
  64.5 0.1 reshape.66
  64.6 0.1 copy.31
  64.6 0.1 pad.3.clone
  64.7 0.7 maximum_maximum_fusion.mine
  65.4 39.3 %shard_map.157 = f32[32,8,384]{2,1,0:T(8,128)} custom-call(f32[8,384]{1,0:T(8,128)} %maximum_maximum_fusion.mine), custom_call_target="tpu_custom_call" | custom-call | tf_op jit(solution)/shard_map/pallas_call | solution.py:341
  104.7 0.9 slice_reduce_fusion
  105.6 1.1 multiply_reduce_fusion
  106.7 0.9 fusion.3
  107.6 0.1 copy.34
  107.7 0.6 fusion.30
  108.3 0.7 dynamic-slice_reduce_fusion
  109.7 0.8 fusion.15
  110.5 0.6 constant_dynamic-slice_fusion
  111.8 0.0 copy-done.5
  111.8 2.1 %fusion = bf16[1024,256]{1,0:T(8,128)(2,1)} fusion(bf16[1024,256]{1,0:T(8,128)(2,1)S(1)} %copy-done.4, pred[1024]{0:T(1024)(128)(4,1)S(1)} %compare_and_fusion, s32[1024]{0:T(1024)S(1)} %add_subtract_fusion, s32[64]{0:T(128)S(1)} %copy-done.5, s32[8]{0:T(128)S(1)} %iota_add_fusion, f32[8,4,8,384]{3,2,1,0:T(8,128)} %bitcast.54), kind=kOutput, calls=%fused_computation.1 | convolution fusion | flops 4991488 | bytes 1086752 | tf_op jit(solution)/shard_map/dot_general | solution.py:438
  (13 shorter events, 0.1 us)
Async XLA Ops:
  0.6 62.7 %copy-start = (bf16[1024,256]{1,0:T(8,128)(2,1)S(1)}, bf16[1024,256]{1,0:T(8,128)(2,1)}, u32[]{:S(2)}) copy-start(bf16[1024,256]{1,0:T(8,128)(2,1)} %param.21) | copy-start | bytes 1572868
  0.6 5.5 %copy-start.2 = (f32[1,1024]{1,0:T(1,128)S(1)}, f32[1,1024]{1,0:T(1,128)}, u32[]{:S(2)}) copy-start(f32[1,1024]{1,0:T(1,128)} %gain_one.1) | copy-start | bytes 12292
  0.7 5.4 %copy-start.3 = (f32[1,1024]{1,0:T(1,128)S(1)}, f32[1,1024]{1,0:T(1,128)}, u32[]{:S(2)}) copy-start(f32[1,1024]{1,0:T(1,128)} %gain_two.1) | copy-start | bytes 12292
  0.7 5.4 %copy-start.1 = (bf16[8,256]{1,0:T(8,128)(2,1)S(1)}, bf16[8,256]{1,0:T(8,128)(2,1)}, u32[]{:S(2)}) copy-start(bf16[8,256]{1,0:T(8,128)(2,1)} %online.1) | copy-start | bytes 12292
  6.1 57.2 %copy-start.6 = (f32[1024]{0:T(1024)S(1)}, f32[1024]{0:T(1024)}, u32[]{:S(2)}) copy-start(f32[1024]{0:T(1024)} %param.20) | copy-start | bytes 12292
  6.1 57.6 %copy-start.4 = (bf16[1024,256]{1,0:T(8,128)(2,1)S(1)}, bf16[1024,256]{1,0:T(8,128)(2,1)}, u32[]{:S(2)}) copy-start(bf16[1024,256]{1,0:T(8,128)(2,1)} %param.23) | copy-start | bytes 1572868
  6.1 105.7 %copy-start.5 = (s32[64]{0:T(128)S(1)}, s32[64]{0:T(128)}, u32[]{:S(2)}) copy-start(s32[64]{0:T(128)} %param.24) | copy-start | bytes 772
